TPU v7x, 32 devices: a whole 2x2x4 slice. The times are simulated.
32 devices in a mesh: ctx: 16 (over z, y, core), head: 2 (over x).
Axes of the slice: x: 2, y: 2, z: 4, core: 2. Of those that a mesh axis runs over, the one named last changes fastest.
Arguments:
- queries: bfloat16 [2048, 8192], P('ctx', 'head'), may hold values from -5.5 to 5.5
- keys: bfloat16 [2048, 1024], P('ctx', 'head'), may hold values from -5.5 to 5.5
- values: bfloat16 [2048, 1024], P('ctx', 'head'), may hold values from -6 to 6
- feature_weights: bfloat16 [64, 128, 64], P('head'), may hold values from -1 to 1
Outputs:
- attn_error: float32 [2048, 8192], P('ctx', 'head')
- loss: float32 [], replicated
- grad_w: float32 [64, 128, 64], P('head')
All inputs are finite; a program needn't handle non-finite values.
Results may differ from a plain program's by a relative error of at most 0.004.
Values may be sent and summed in bfloat16 or wider, within the bound.
No kernel may reach another device: no remote copies, remote signals or barrier semaphores. Data moves between devices by JAX's collectives and lax.ppermute only.
A program may use at most 192 MiB of HBM per device.

v0:
```python
import math
import jax
import jax.numpy as jnp
from jax import lax
from jax.sharding import PartitionSpec as P

HEAD_SIZE = 128
QUERY_HEADS = 64
KEY_VALUE_HEADS = 8
FM = 64
WIN = 64
phi_scale = 0.00390625
big_negative = -1e30
highest = lax.Precision.HIGHEST


def swapped(value, axis, distance):
    mask = 2**distance
    pairs = [(source, source ^ mask) for source in range(lax.axis_size(axis))]
    return lax.ppermute(value, axis, pairs)


def carried_in(value, axis, combine, identity):
    devices, here = (lax.axis_size(axis), lax.axis_index(axis))
    everything = jax.tree.map(
        lambda part, kind: lax.all_gather(part.astype(kind), axis),
        value,
        (jnp.bfloat16, jnp.bfloat16),
    )
    start = jax.tree.map(
        lambda part, zero: jnp.broadcast_to(jnp.asarray(zero, part.dtype), part.shape),
        value,
        identity,
    )

    def carried_step(k, before):
        reached = k < here
        new = combine(
            before, jax.tree.map(lambda part, own: part[k].astype(own.dtype), everything, value)
        )
        return jax.tree.map(lambda a, b: jnp.where(reached, a, b), new, before)

    return lax.fori_loop(0, devices, carried_step, start)


def prefix(value, axis, combine, identity):
    devices, here = (lax.axis_size(axis), lax.axis_index(axis))
    everything = jax.tree.map(
        lambda part, kind: lax.all_gather(part.astype(kind), axis),
        value,
        jax.tree.map(lambda a: jnp.bfloat16 if a.dtype == jnp.float32 else a.dtype, value),
    )
    start = jax.tree.map(
        lambda part, zero: jnp.broadcast_to(jnp.asarray(zero, part.dtype), part.shape),
        value,
        identity,
    )

    def prefix_step(k, before):
        at = devices - 1 - k
        reached = at > here
        new = combine(
            before, jax.tree.map(lambda part, own: part[at].astype(own.dtype), everything, value)
        )
        return jax.tree.map(lambda a, b: jnp.where(reached, a, b), new, before)

    return lax.fori_loop(0, devices, prefix_step, start)


def features(projection):
    return phi_scale * jnp.concatenate(
        [1.0 + jax.nn.elu(projection), 1.0 + jax.nn.elu(-projection)], axis=-1
    )


def feature_back(projection, grad_phi):
    half = projection.shape[-1]
    slope_plus = jnp.where(projection > 0, 1.0, jnp.exp(jnp.minimum(projection, 0.0)))
    slope_minus = jnp.where(projection < 0, 1.0, jnp.exp(jnp.minimum(-projection, 0.0)))
    return phi_scale * (grad_phi[..., :half] * slope_plus - grad_phi[..., half:] * slope_minus)


def add_pair(earlier, later):
    return (earlier[0] + later[0], earlier[1] + later[1])


def split_product(form, phi_part, data):
    upper = phi_part.astype(jnp.bfloat16)
    lower = (phi_part - upper.astype(jnp.float32)).astype(jnp.bfloat16)
    return jnp.einsum(form, upper, data, preferred_element_type=jnp.float32) + jnp.einsum(
        form, lower, data, preferred_element_type=jnp.float32
    )


def visit_partner(rows):
    for bit_index in range(lax.axis_size("ctx").bit_length() - 1):
        rows = swapped(rows, "ctx", bit_index)
    return rows


def return_partner(rows):
    for bit_index in range(lax.axis_size("ctx").bit_length() - 1):
        rows = swapped(rows.astype(jnp.bfloat16), "ctx", bit_index).astype(rows.dtype)
    return rows


def teacher_part(part, query_set, pos_set, key_block, value_block, key_pos, masked):
    scale_factor = 1.0 / math.sqrt(query_set.shape[-1])
    scores = (
        jnp.einsum("qgrd,kgd->grqk", query_set, key_block, preferred_element_type=jnp.float32)
        * scale_factor
    )
    if masked:
        causal = key_pos[None, :] <= pos_set[:, None]
        top = jnp.maximum(part[0], jnp.max(jnp.where(causal, scores, big_negative), axis=-1))
        weights = jnp.exp(jnp.where(causal, scores - top[..., None], big_negative))
    else:
        top = jnp.maximum(part[0], jnp.max(scores, axis=-1))
        weights = jnp.exp(scores - top[..., None])
    rescale = jnp.exp(part[0] - top)
    total = part[1] * rescale + jnp.sum(weights, axis=-1)
    mixed = part[2] * rescale[..., None] + jnp.einsum(
        "grqk,kgd->grqd",
        weights.astype(jnp.bfloat16),
        value_block,
        preferred_element_type=jnp.float32,
    )
    return (top, total, mixed)


def advance(part, row_set, key_block, value_block, key_pos, first):
    query_set, pos_set = row_set
    needed = first <= pos_set[-1]
    straddle = key_pos[-1] > pos_set[0]
    branch_index = jnp.where(needed, jnp.where(straddle, 2, 1), 0).astype(jnp.int32)
    return lax.switch(
        branch_index,
        [
            lambda current: current,
            lambda current: teacher_part(
                current, query_set, pos_set, key_block, value_block, key_pos, False
            ),
            lambda current: teacher_part(
                current, query_set, pos_set, key_block, value_block, key_pos, True
            ),
        ],
        part,
    )


def shards(queries, keys, values, feature_weights):
    local_rows = queries.shape[0]
    half_rows = local_rows // 2
    groups = keys.shape[1] // HEAD_SIZE
    group_ratio = QUERY_HEADS // KEY_VALUE_HEADS
    heads_here = groups * group_ratio
    ctx_count = lax.axis_size("ctx")
    ctx_place = lax.axis_index("ctx")
    own_start = ctx_place * local_rows
    query4 = queries.reshape(local_rows, groups, group_ratio, HEAD_SIZE)
    own_keys = keys.reshape(local_rows, groups, HEAD_SIZE)
    own_values = values.reshape(local_rows, groups, HEAD_SIZE)
    weight4 = feature_weights.reshape(groups, group_ratio, HEAD_SIZE, FM)
    scale = 1.0 / math.sqrt(HEAD_SIZE)
    query_pos = own_start + jnp.arange(local_rows, dtype=jnp.int32)
    tail_offsets = jnp.arange(WIN, dtype=jnp.int32)
    proj_own = jnp.einsum("kgd,grdf->grkf", own_keys, weight4, preferred_element_type=jnp.float32)
    first_set = (query4[:half_rows], query_pos[:half_rows])
    partner_start = (ctx_count - 1 - ctx_place) * local_rows
    visiting = visit_partner(query4[half_rows:])
    second_set = (visiting, partner_start + half_rows + jnp.arange(half_rows, dtype=jnp.int32))
    row_sets = (first_set, second_set)

    def add_tail(tails, key_block, value_block, key_pos):
        pick = (key_pos[None, :] == own_start - WIN + tail_offsets[:, None]).astype(jnp.bfloat16)
        return (
            tails[0]
            + jnp.einsum("wk,kgd->wgd", pick, key_block, preferred_element_type=jnp.float32),
            tails[1]
            + jnp.einsum("wk,kgd->wgd", pick, value_block, preferred_element_type=jnp.float32),
        )

    part_zero = (
        jnp.full((groups, group_ratio, half_rows), big_negative, jnp.float32),
        jnp.zeros((groups, group_ratio, half_rows), jnp.float32),
        jnp.zeros((groups, group_ratio, half_rows, HEAD_SIZE), jnp.float32),
    )
    tail_zero = (
        jnp.zeros((WIN, groups, HEAD_SIZE), jnp.float32),
        jnp.zeros((WIN, groups, HEAD_SIZE), jnp.float32),
    )
    state_zero = (
        jnp.zeros((groups, group_ratio, 2 * FM, HEAD_SIZE), jnp.float32),
        jnp.zeros((groups, group_ratio, 2 * FM), jnp.float32),
    )
    carry = ((part_zero, part_zero), tail_zero, ())
    key_piece = lax.all_gather(keys, "ctx", axis=0, tiled=True)
    value_piece = lax.all_gather(values, "ctx", axis=0, tiled=True)
    piece_rows = key_piece.shape[0]
    stride = math.gcd(piece_rows, local_rows)
    count = piece_rows // stride
    key_blocks = key_piece.reshape(count, stride, groups, HEAD_SIZE)
    value_blocks = value_piece.reshape(count, stride, groups, HEAD_SIZE)

    def fold_step(state, inputs):
        key_block, value_block, number = inputs
        first = number * stride
        key_pos = first + jnp.arange(stride, dtype=jnp.int32)
        parts_now, tails_now, states_now = state
        new_parts = (
            advance(parts_now[0], row_sets[0], key_block, value_block, key_pos, first),
            advance(parts_now[1], row_sets[1], key_block, value_block, key_pos, first),
        )
        earlier_block = first < own_start
        new_tails = lax.cond(
            earlier_block,
            lambda current: add_tail(current, key_block, value_block, key_pos),
            lambda current: current,
            tails_now,
        )
        return ((new_parts, new_tails, states_now), None)

    carry, unused = lax.scan(
        fold_step, carry, (key_blocks, value_blocks, jnp.arange(count, dtype=jnp.int32))
    )
    phi_own = features(proj_own)
    local_kv = split_product("grkf,kgd->grfd", phi_own, own_values)
    state_kv, state_norm = carried_in(
        (local_kv, jnp.sum(phi_own, axis=2)), "ctx", add_pair, state_zero
    )
    parts_done, tails_done = (carry[0], carry[1])
    teacher_first = parts_done[0][2] / parts_done[0][1][..., None]
    teacher_second = parts_done[1][2] / parts_done[1][1][..., None]
    teacher_second = return_partner(teacher_second)
    teacher = jnp.concatenate([teacher_first, teacher_second], axis=2)
    tail_key = tails_done[0].astype(jnp.bfloat16)
    tail_value = tails_done[1].astype(jnp.bfloat16)
    slab_key = jnp.concatenate([tail_key, own_keys], axis=0)
    slab_value = jnp.concatenate([tail_value, own_values], axis=0).astype(jnp.float32)
    slab_rows = WIN + local_rows
    slab_pos = own_start - WIN + jnp.arange(slab_rows, dtype=jnp.int32)
    is_tail = jnp.arange(slab_rows, dtype=jnp.int32) < WIN
    proj_tail = jnp.einsum("kgd,grdf->grkf", tail_key, weight4, preferred_element_type=jnp.float32)
    proj_slab = jnp.concatenate([proj_tail, proj_own], axis=2)
    phi_slab = features(proj_slab)
    proj_query = jnp.einsum("qgrd,grdf->grqf", query4, weight4, preferred_element_type=jnp.float32)
    phi_query = features(proj_query)
    scores = (
        jnp.einsum("qgrd,kgd->grqk", query4, slab_key, preferred_element_type=jnp.float32) * scale
    )
    window = (
        (slab_pos[None, :] >= query_pos[:, None] - WIN)
        & (slab_pos[None, :] <= query_pos[:, None])
        & (slab_pos[None, :] >= 0)
    )
    far = jnp.logical_not(is_tail)[None, :] & (slab_pos[None, :] < query_pos[:, None] - WIN)
    coefficient = far.astype(jnp.float32) - (window & is_tail[None, :]).astype(jnp.float32)
    window_top = jnp.max(jnp.where(window, scores, big_negative), axis=-1)
    local = jnp.exp(jnp.where(window, scores - window_top[..., None], big_negative))
    kernel = jnp.einsum("grqf,grkf->grqk", phi_query, phi_slab, precision=highest)
    mixed = local + coefficient * kernel
    numerator = jnp.einsum("grqk,kgd->grqd", mixed, slab_value, precision=highest) + jnp.einsum(
        "grqf,grfd->grqd", phi_query, state_kv, precision=highest
    )
    denominator = jnp.sum(mixed, axis=-1) + jnp.einsum(
        "grqf,grf->grq", phi_query, state_norm, precision=highest
    )
    student = numerator / denominator[..., None]
    error = student - teacher
    attn_error = jnp.transpose(error, (2, 0, 1, 3)).reshape(local_rows, heads_here * HEAD_SIZE)
    whole_rows = local_rows * ctx_count
    loss = lax.psum(jnp.sum(error * error), ("ctx", "head")) / (whole_rows * QUERY_HEADS)
    grad_out = 2.0 * error / denominator[..., None]
    grad_den = -jnp.sum(grad_out * student, axis=-1)
    later_kv = jnp.einsum("grqf,grqd->grfd", phi_query, grad_out, precision=highest)
    later_norm = jnp.einsum("grqf,grq->grf", phi_query, grad_den, precision=highest)
    suffix_kv, suffix_norm = prefix((later_kv, later_norm), "ctx", add_pair, state_zero)
    grad_lin = coefficient * (
        jnp.einsum("grqd,kgd->grqk", grad_out, slab_value, precision=highest) + grad_den[..., None]
    )
    grad_phi_query = (
        jnp.einsum("grqk,grkf->grqf", grad_lin, phi_slab, precision=highest)
        + jnp.einsum("grqd,grfd->grqf", grad_out, state_kv, precision=highest)
        + grad_den[..., None] * state_norm[:, :, None, :]
    )
    grad_phi_slab = jnp.einsum("grqk,grqf->grkf", grad_lin, phi_query, precision=highest)
    own_extra = (
        jnp.einsum("kgd,grfd->grkf", own_values.astype(jnp.float32), suffix_kv, precision=highest)
        + suffix_norm[:, :, None, :]
    )
    grad_phi_slab = grad_phi_slab + jnp.concatenate(
        [jnp.zeros((groups, group_ratio, WIN, 2 * FM), jnp.float32), own_extra], axis=2
    )
    grad_proj_query = feature_back(proj_query, grad_phi_query)
    grad_proj_slab = feature_back(proj_slab, grad_phi_slab)
    grad_local = jnp.einsum(
        "qgrd,grqf->grdf", query4.astype(jnp.float32), grad_proj_query, precision=highest
    ) + jnp.einsum(
        "kgd,grkf->grdf", slab_key.astype(jnp.float32), grad_proj_slab, precision=highest
    )
    grad_w = lax.psum(grad_local.reshape(heads_here, HEAD_SIZE, FM), "ctx")
    return (attn_error, loss, grad_w)


def solution(mesh):
    placed = (P("ctx", "head"), P("ctx", "head"), P("ctx", "head"), P("head", None, None))
    return jax.shard_map(
        shards,
        mesh=mesh,
        in_specs=placed,
        out_specs=(P("ctx", "head"), P(), P("head", None, None)),
        check_vma=False,
    )
```

profile of v0, /device:TPU:0, one launch (start us, length us, event | category | flops | bytes accessed | tf_op | source)
XLA Modules:
  0.0 783.3 jit_solution(9861084651910707477)
XLA Ops:
  29.9 8.6 %collective-permute-done.1 = bf16[64,4,8,128]{3,2,1,0:T(8,128)(2,1)} collective-permute-done((bf16[64,4,8,128]{3,2,1,0:T(8,128)(2,1)}, bf16[64,4,8,128]{3,2,1,0:T(8,128)(2,1)}, u32[]{:S(2)}, u32[]{:S(2)}) %collective-permute-start.1) | collective-permute-done | bytes 524320 | tf_op jit(solution)/shard_map/ppermute | solution.py:20
  40.3 5.5 fusion.79
  45.8 13.8 %collective-permute-done.2 = bf16[64,4,8,128]{3,2,1,0:T(8,128)(2,1)} collective-permute-done((bf16[64,4,8,128]{3,2,1,0:T(8,128)(2,1)}, bf16[64,4,8,128]{3,2,1,0:T(8,128)(2,1)}, u32[]{:S(2)}, u32[]{:S(2)}) %collective-permute-start.2) | collective-permute-done | bytes 524320 | tf_op jit(solution)/shard_map/ppermute | solution.py:20
  68.9 20.4 %collective-permute-done.3 = bf16[64,4,8,128]{3,2,1,0:T(8,128)(2,1)} collective-permute-done((bf16[64,4,8,128]{3,2,1,0:T(8,128)(2,1)}, bf16[64,4,8,128]{3,2,1,0:T(8,128)(2,1)}, u32[]{:S(2)}, u32[]{:S(2)}) %collective-permute-start.3) | collective-permute-done | bytes 524320 | tf_op jit(solution)/shard_map/ppermute | solution.py:20
  95.8 16.4 %all-gather.11.cloned.1.call-done = bf16[2048,512]{1,0:T(8,128)(2,1)} async-done(((bf16[128,512]{1,0:T(8,128)(2,1)}), bf16[2048,512]{1,0:T(8,128)(2,1)}) %all-gather.11.cloned.1.call-update) | async-done | bytes 2097168 | tf_op jit(solution)/shard_map/all_gather | solution.py:198
  118.3 193.6 %while.59 = (s32[]{:T(128)}, f32[4,8,64]{2,1,0:T(8,128)S(1)}, f32[4,8,64]{2,1,0:T(8,128)S(1)}, f32[4,8,64,128]{3,2,1,0:T(8,128)S(1)}, f32[4,8,64]{2,1,0:T(8,128)...) while((s32[]{:T(128)}, f32[4,8,64]{2,1,0:T(8,128)S(1)}, ...), condition=%wide.region_17.18_spmd.clone, body=%wide.region_0.17_spmd.clone.sunk | while | flops 291086528 | bytes 14226523 | solution.py:223
  316.5 64.0 %all-gather.1 = bf16[64,8,128]{2,1,0:T(8,128)(2,1)} all-gather(bf16[4,8,128]{2,1,0:T(8,128)(2,1)S(1)} %fusion.143), channel_id=3, replica_groups=mesh['ctx'=16,'head'=2] {'ctx'}, dimensions={0}, use_global_device_ids=true | all-gather | bytes 139264 | tf_op jit(solution)/shard_map/all_gather | solution.py:26
  389.1 4.7 fusion.109
  393.8 4.8 collective-permute-done.5
  400.9 11.1 %collective-permute-done.6 = bf16[4,8,64,128]{3,2,1,0:T(8,128)(2,1)S(1)} collective-permute-done((bf16[4,8,64,128]{3,2,1,0:T(8,128)(2,1)S(1)}, bf16[4,8,64,128]{3,2,1,0:T(8,128)(2,1)S(1)}, u32[]{:S(2)}, u32[]{:S(2)}) %collective-permute-start.6) | collective-permute-done | bytes 524320 | tf_op jit(solution)/shard_map/ppermute | solution.py:20
  413.3 5.2 fusion.122
  418.5 18.1 %collective-permute-done.7 = bf16[4,8,64,128]{3,2,1,0:T(8,128)(2,1)S(1)} collective-permute-done((bf16[4,8,64,128]{3,2,1,0:T(8,128)(2,1)S(1)}, bf16[4,8,64,128]{3,2,1,0:T(8,128)(2,1)S(1)}, u32[]{:S(2)}, u32[]{:S(2)}) %collective-permute-start.7) | collective-permute-done | bytes 524320 | tf_op jit(solution)/shard_map/ppermute | solution.py:20
  437.7 49.1 %while.60 = (s32[]{:T(128)}, f32[4,8,128,128]{3,2,1,0:T(8,128)S(1)}, f32[4,8,128]{2,1,0:T(8,128)S(1)}, s32[]{:T(128)}, bf16[16,4,8,128,128]{4,3,2,1,0:T(8,128)(2...) while((s32[]{:T(128)}, f32[4,8,128,128]{3,2,1,0:T(8,128)S(1)}, ...), condition=%wide.region_21.22_spmd.clone, body=%wide.region_20.21_spmd.clone.sunk | while | flops 2113540 | bytes 5283955 | solution.py:43
  486.7 5.7 fusion.150
  492.5 6.4 multiply_reduce_fusion
  509.0 19.1 %all-gather.3 = bf16[64,8,128]{2,1,0:T(8,128)(2,1)S(1)} all-gather(bf16[4,8,128]{2,1,0:T(8,128)(2,1)S(1)} %convert_element_type.142), channel_id=5, replica_groups=mesh['ctx'=16,'head'=2] {'ctx'}, dimensions={0}, use_global_device_ids=true | all-gather | bytes 139264 | tf_op jit(solution)/shard_map/all_gather | solution.py:49
  531.3 7.9 %fusion.68 = f32[4,8,128,128]{3,2,1,0:T(8,128)S(1)} fusion(f32[4,8,128,192]{2,3,1,0:T(8,128)S(1)} %fusion.121, f32[4,8,128]{2,1,0:T(8,128)S(1)} %neg.21, f32[128,192]{0,1:T(8,128)S(1)} %convert_subtract_fusion, f32[4,8,192,64]{3,2,1,0:T(8,128)S(1)} %copy-done.11, f32[4,8,192,64]{3,2,1,0:T(8,128)S(1)} %copy-done.9), kind=kOutput, calls=%fused_computation.116 | convolution fusion | flops 1211105280 | bytes 8503296 | tf_op jit(solution)/shard_map/grqk,grkf->grqf/dot_general | solution.py:282
  539.2 4.8 multiply_add_fusion.4
  548.6 81.4 %all-gather.15.cloned.1.call-done = bf16[64,8,128,128]{3,2,1,0:T(8,128)(2,1)} async-done(((bf16[4,8,128,128]{3,2,1,0:T(8,128)(2,1)}), bf16[64,8,128,128]{3,2,1,0:T(8,128)(2,1)}) %all-gather.15.cloned.1.call-update) | async-done | bytes 16777232 | tf_op jit(solution)/shard_map/all_gather | solution.py:49
  630.0 38.6 %while.61 = (s32[]{:T(128)}, f32[4,8,128,128]{3,2,1,0:T(8,128)S(1)}, f32[4,8,128]{2,1,0:T(8,128)S(1)}, s32[]{:T(128)}, bf16[16,4,8,128,128]{4,3,2,1,0:T(8,128)(2...) while((s32[]{:T(128)}, ...), condition=%wide.region_27.28_spmd.clone, body=%wide.region_26.27_spmd.clone.sunk | while | flops 2113544 | bytes 5284017 | solution.py:67
  670.2 5.7 pad_add_fusion
  675.9 5.3 fusion.102
  681.2 39.0 %psum.14 = f32[]{:T(128)} all-reduce(f32[]{:T(128)} %get-tuple-element.673), channel_id=1, replica_groups=mesh['ctx'=16,'head'=2] {'ctx','head'}, use_global_device_ids=true, to_apply=%region_24.25 | all-reduce | flops 1 | bytes 8 | tf_op jit(solution)/shard_map/psum | solution.py:272
  724.6 48.3 %all-reduce.3.cloned.1.call-done = f32[32,128,64]{1,2,0:T(8,128)} async-done(((f32[32,128,64]{1,2,0:T(8,128)}), f32[32,128,64]{1,2,0:T(8,128)}) %all-reduce.3.cloned.1.call-update) | async-done | bytes 1048592 | tf_op jit(solution)/shard_map/psum | solution.py:301
  (491 shorter events, 355.4 us)
Async XLA Ops:
  7.2 84.2 %all-gather.9.cloned.1.call-start = ((), (), s32[]{:S(2)}) async-start(), calls=%async_computation | async-start | bytes 2228224 | tf_op jit(solution)/shard_map/all_gather | solution.py:197
  7.9 104.2 %all-gather.11.cloned.1.call-start = ((), (), s32[]{:S(2)}) async-start(), calls=%async_computation.1 | async-start | bytes 2228224 | tf_op jit(solution)/shard_map/all_gather | solution.py:198
  8.7 429.0 %all-gather.13.cloned.1.call-start = ((), (), s32[]{:S(2)}) async-start(), calls=%async_computation.3 | async-start | bytes 17825792 | tf_op jit(solution)/shard_map/all_gather | solution.py:26
  10.8 53.0 %copy-start.22 = (bf16[128,512]{0,1:T(8,128)(2,1)}, bf16[128,512]{0,1:T(8,128)(2,1)S(1)}, u32[]{:S(2)}) copy-start(bf16[128,512]{0,1:T(8,128)(2,1)S(1)} %copy.138) | copy-start | bytes 393220
  17.9 612.1 %all-gather.15.cloned.1.call-start = ((), (), s32[]{:S(2)}) async-start(), calls=%async_computation.4 | async-start | bytes 17825792 | tf_op jit(solution)/shard_map/all_gather | solution.py:49
  20.1 2.9 collective-permute-start
  23.1 15.4 %collective-permute-start.1 = (bf16[64,4,8,128]{3,2,1,0:T(8,128)(2,1)}, bf16[64,4,8,128]{3,2,1,0:T(8,128)(2,1)}, u32[]{:S(2)}, u32[]{:S(2)}) collective-permute-start(bf16[64,4,8,128]{3,2,1,0:T(8,128)(2,1)} %collective-permute-done), channel_id=1, source_target_pairs={{0,4},{2,6},{4,0},{6,2},{8,12},{10,14},{12,8},{14,10},{16,20},{18,... | collective-permute-start | bytes 1572872 | tf_op jit(solution)/shard_map/ppermute | solution.py:20
  29.9 16.0 %copy-start.28 = (u8[4,128,64]{2,1,0:T(8,128)(4,1)}, u8[4,128,64]{2,1,0:T(8,128)(4,1)S(1)}, u32[]{:S(2)}) copy-start(u8[4,128,64]{2,1,0:T(8,128)(4,1)S(1)} %get-tuple-element.671) | copy-start | bytes 98308
  38.5 21.1 %collective-permute-start.2 = (bf16[64,4,8,128]{3,2,1,0:T(8,128)(2,1)}, bf16[64,4,8,128]{3,2,1,0:T(8,128)(2,1)}, u32[]{:S(2)}, u32[]{:S(2)}) collective-permute-start(bf16[64,4,8,128]{3,2,1,0:T(8,128)(2,1)} %collective-permute-done.1), channel_id=1, source_target_pairs={{0,8},{2,10},{4,12},{6,14},{8,0},{10,2},{12,4},{14,6},{16,24},{18,... | collective-permute-start | bytes 1572872 | tf_op jit(solution)/shard_map/ppermute | solution.py:20
  40.3 21.7 %copy-start.14 = (f32[4,8,128,64]{3,2,1,0:T(8,128)S(1)}, f32[4,8,128,64]{3,2,1,0:T(8,128)}, u32[]{:S(2)}) copy-start(f32[4,8,128,64]{3,2,1,0:T(8,128)} %copy-done.13) | copy-start | bytes 3145732
  59.6 29.8 %collective-permute-start.3 = (bf16[64,4,8,128]{3,2,1,0:T(8,128)(2,1)}, bf16[64,4,8,128]{3,2,1,0:T(8,128)(2,1)}, u32[]{:S(2)}, u32[]{:S(2)}) collective-permute-start(bf16[64,4,8,128]{3,2,1,0:T(8,128)(2,1)} %collective-permute-done.2), channel_id=1, source_target_pairs={{0,16},{2,18},{4,20},{6,22},{8,24},{10,26},{12,28},{14,30},{16,0},... | collective-permute-start | bytes 1572872 | tf_op jit(solution)/shard_map/ppermute | solution.py:20
  313.0 71.4 %collective-permute-start.4 = (bf16[4,8,64,128]{3,2,1,0:T(8,128)(2,1)}, bf16[4,8,64,128]{3,2,1,0:T(8,128)(2,1)S(1)}, u32[]{:S(2)}, u32[]{:S(2)}) collective-permute-start(bf16[4,8,64,128]{3,2,1,0:T(8,128)(2,1)} %divide_convert_fusion), channel_id=1, source_target_pairs={{0,2},{2,0},{4,6},{6,4},{8,10},{10,8},{12,14},{14,12},{16,18},{18,... | collective-permute-start | bytes 1572872 | tf_op jit(solution)/shard_map/ppermute | solution.py:20
  384.4 14.2 %collective-permute-start.5 = (bf16[4,8,64,128]{3,2,1,0:T(8,128)(2,1)S(1)}, bf16[4,8,64,128]{3,2,1,0:T(8,128)(2,1)S(1)}, u32[]{:S(2)}, u32[]{:S(2)}) collective-permute-start(bf16[4,8,64,128]{3,2,1,0:T(8,128)(2,1)S(1)} %collective-permute-done.4), channel_id=1, source_target_pairs={{0,4},{2,6},{4,0},{6,2},{8,12},{10,14},{12,8},{14,10},{16,20},{18,... | collective-permute-start | bytes 1572872 | tf_op jit(solution)/shard_map/ppermute | solution.py:20
  389.1 9.6 %copy-start.20 = (bf16[16,8,32,128]{3,2,1,0:T(8,128)(2,1)S(1)}, bf16[16,8,32,128]{3,2,1,0:T(8,128)(2,1)}, u32[]{:S(2)}) copy-start(bf16[16,8,32,128]{3,2,1,0:T(8,128)(2,1)} %copy.204) | copy-start | bytes 3145732
  389.1 9.6 %copy-start.27 = (bf16[128,4,128]{2,0,1:T(8,128)(2,1)S(1)}, bf16[128,4,128]{2,0,1:T(8,128)(2,1)}, u32[]{:S(2)}) copy-start(bf16[128,4,128]{2,0,1:T(8,128)(2,1)} %copy.128) | copy-start | bytes 393220
  398.6 13.4 %collective-permute-start.6 = (bf16[4,8,64,128]{3,2,1,0:T(8,128)(2,1)S(1)}, bf16[4,8,64,128]{3,2,1,0:T(8,128)(2,1)S(1)}, u32[]{:S(2)}, u32[]{:S(2)}) collective-permute-start(bf16[4,8,64,128]{3,2,1,0:T(8,128)(2,1)S(1)} %collective-permute-done.5), channel_id=1, source_target_pairs={{0,8},{2,10},{4,12},{6,14},{8,0},{10,2},{12,4},{14,6},{16,24},{18,... | collective-permute-start | bytes 1572872 | tf_op jit(solution)/shard_map/ppermute | solution.py:20
  400.9 12.4 %copy-start.26 = (bf16[128,4,128]{2,0,1:T(8,128)(2,1)S(1)}, bf16[128,4,128]{2,0,1:T(8,128)(2,1)}, u32[]{:S(2)}) copy-start(bf16[128,4,128]{2,0,1:T(8,128)(2,1)} %copy.139) | copy-start | bytes 393220
  412.0 24.6 %collective-permute-start.7 = (bf16[4,8,64,128]{3,2,1,0:T(8,128)(2,1)S(1)}, bf16[4,8,64,128]{3,2,1,0:T(8,128)(2,1)S(1)}, u32[]{:S(2)}, u32[]{:S(2)}) collective-permute-start(bf16[4,8,64,128]{3,2,1,0:T(8,128)(2,1)S(1)} %collective-permute-done.6), channel_id=1, source_target_pairs={{0,16},{2,18},{4,20},{6,22},{8,24},{10,26},{12,28},{14,30},{16,0},... | collective-permute-start | bytes 1572872 | tf_op jit(solution)/shard_map/ppermute | solution.py:20
  413.3 24.3 %copy-start.2 = (f32[4,8,128,128]{3,2,1,0:T(8,128)S(1)}, f32[4,8,128,128]{3,2,1,0:T(8,128)}, u32[]{:S(2)}) copy-start(f32[4,8,128,128]{3,2,1,0:T(8,128)} %custom-call) | copy-start | bytes 6291460
  486.7 12.1 %copy-start.3 = (f32[4,8,128,128]{3,2,1,0:T(8,128)}, f32[4,8,128,128]{3,2,1,0:T(8,128)S(1)}, u32[]{:S(2)}) copy-start(f32[4,8,128,128]{3,2,1,0:T(8,128)S(1)} %get-tuple-element.496) | copy-start | bytes 6291460
  504.8 268.1 %all-reduce.3.cloned.1.call-start = ((), (), s32[]{:S(2)}) async-start(), calls=%async_computation.2 | async-start | bytes 2097152 | tf_op jit(solution)/shard_map/psum | solution.py:301
  505.3 25.9 %copy-start.11 = (f32[4,8,192,64]{3,2,1,0:T(8,128)S(1)}, f32[4,8,192,64]{3,2,1,0:T(8,128)}, u32[]{:S(2)}) copy-start(f32[4,8,192,64]{3,2,1,0:T(8,128)} %copy-done.10) | copy-start | bytes 4718596
  630.0 38.6 %copy-start.23 = (bf16[128,512]{0,1:T(8,128)(2,1)S(1)}, bf16[128,512]{0,1:T(8,128)(2,1)}, u32[]{:S(2)}) copy-start(bf16[128,512]{0,1:T(8,128)(2,1)} %copy-done.22) | copy-start | bytes 393220
  722.1 53.1 %copy-start.1 = (bf16[32,128,64]{1,2,0:T(8,128)(2,1)S(1)}, bf16[32,128,64]{1,2,0:T(8,128)(2,1)}, u32[]{:S(2)}) copy-start(bf16[32,128,64]{1,2,0:T(8,128)(2,1)} %param.21) | copy-start | bytes 1572868
  (21 other events, 101.3 us)
Sparse Core Ops, SparseCore 0:
  10.2 45.6 all-gather.8
  58.0 54.1 all-gather.10
  114.3 125.7 all-gather.12
  505.0 124.9 all-gather.14
  681.3 91.5 all-reduce.2
where the time goes:
time: 796 us; the launch traced here: 783 us
  waiting for transfers between devices  224 us (28%)
  blocking collectives  122 us (15%)
  matrix products  120 us (15%)
  other arithmetic  120 us (15%)
  local copies, waits for them, and re-layouts  96.2 us (12%)
  loops' own time  72.7 us (9%)
  between operations  16.5 us (2%)
  starting transfers between devices  11 us (1%)
    all_gather x1, waiting for transfers between devices, prefix(): lax.all_gather(part.astype(kind), axis)  81.4 us
    ppermute x8, waiting for transfers between devices, swapped(): return lax.ppermute(value, axis, pairs)  76.8 us
    another operation x1, loops' own time, shards(): lax.scan(fold_step, carry, (key_blocks, value_blocks, jnp.arange(count, d...  70.5 us
    all_gather x1, blocking collectives, carried_in(): lax.all_gather(part.astype(kind), axis)  64 us
    select_n x32, other arithmetic, carried_step(): return jax.tree.map(lambda a, b: jnp.where(reached, a, b), new, before)  49 us
    psum x1, waiting for transfers between devices, shards(): grad_w = lax.psum(grad_local.reshape(heads_here, HEAD_SIZE, FM), 'ctx')  48.3 us
    psum x1, blocking collectives, shards(): lax.psum(jnp.sum(error * error), ('ctx', 'head'))  39 us
    dynamic_slice x64, local copies, waits for them, and re-layouts, shards(): lax.scan(fold_step, carry, (key_blocks, value_blocks, jnp.arange(count, d...  38.7 us
  transfers between devices with their start and end apart: 13, of which 9 were waited for; matrix products, arithmetic and copies ran while one was open for 28% of the time, Pallas kernels for 0%

commit v1 on v0

--- a/solution.py
+++ b/solution.py
@@ -12,6 +12,11 @@
 phi_scale = 0.00390625
 big_negative = -1e30
 highest = lax.Precision.HIGHEST
+
+
+def deliver_ports_in(local_x, local_values):
+    tall = jnp.concatenate([local_x, local_values], axis=1)
+    return jnp.split(lax.all_gather(tall, "ctx", tiled=True, axis=0), [local_x.shape[1]], axis=1)
 
 
 def swapped(value, axis, distance):
@@ -194,8 +199,7 @@
         jnp.zeros((groups, group_ratio, 2 * FM), jnp.float32),
     )
     carry = ((part_zero, part_zero), tail_zero, ())
-    key_piece = lax.all_gather(keys, "ctx", axis=0, tiled=True)
-    value_piece = lax.all_gather(values, "ctx", axis=0, tiled=True)
+    key_piece, value_piece = deliver_ports_in(keys, values)
     piece_rows = key_piece.shape[0]
     stride = math.gcd(piece_rows, local_rows)
     count = piece_rows // stride

time: 796 us -> 825 us (1.036)
  local copies, waits for them, and re-layouts: 96.2 us -> 113 us
  waiting for transfers between devices: 224 us -> 238 us
    ppermute x8, waiting for transfers between devices: 76.8 us -> 108 us  [swapped(): return lax.ppermute(value, axis, pairs)]
    all_gather x2 -> x1, waiting for transfers between devices: 16.4 us -> 0.01 us  [deliver_ports_in(): lax.all_gather(tall, 'ctx', tiled=True, axis=0)]
    reshape x1, local copies, waits for them, and re-layouts: 4.4 us -> 16.5 us  [shards(): key_blocks = key_piece.reshape(count, stride, groups, HEAD_SIZE)]
  transfers between devices with their start and end apart: 13 -> 12, of which waited for: 9 -> 8; matrix products, arithmetic and copies ran while one was open for 28% -> 29% of each run, Pallas kernels for 0% -> 0%
where the time goes in v1:
time: 825 us; the launch traced here: 812 us
  waiting for transfers between devices  238 us (29%)
  other arithmetic  122 us (15%)
  blocking collectives  122 us (15%)
  matrix products  120 us (15%)
  local copies, waits for them, and re-layouts  113 us (14%)
  loops' own time  72.1 us (9%)
  between operations  16.5 us (2%)
  starting transfers between devices  8.31 us (1%)
    ppermute x8, waiting for transfers between devices, swapped(): return lax.ppermute(value, axis, pairs)  108 us
    all_gather x1, waiting for transfers between devices, prefix(): lax.all_gather(part.astype(kind), axis)  81.3 us
    another operation x1, loops' own time, shards(): lax.scan(fold_step, carry, (key_blocks, value_blocks, jnp.arange(count, d...  70 us
    all_gather x1, blocking collectives, carried_in(): lax.all_gather(part.astype(kind), axis)  64.2 us
    select_n x32, other arithmetic, carried_step(): return jax.tree.map(lambda a, b: jnp.where(reached, a, b), new, before)  49 us
    psum x1, waiting for transfers between devices, shards(): grad_w = lax.psum(grad_local.reshape(heads_here, HEAD_SIZE, FM), 'ctx')  48.3 us
    psum x1, blocking collectives, shards(): lax.psum(jnp.sum(error * error), ('ctx', 'head'))  39 us
    select_n x32, other arithmetic, prefix_step(): return jax.tree.map(lambda a, b: jnp.where(reached, a, b), new, before)  38 us
  transfers between devices with their start and end apart: 12, of which 8 were waited for; matrix products, arithmetic and copies ran while one was open for 29% of the time, Pallas kernels for 0%

profile of v1, /device:TPU:0, one launch (start us, length us, event | category | flops | bytes accessed | tf_op | source)
XLA Modules:
  0.0 812.5 jit_solution(16124239268378740649)
XLA Ops:
  30.2 8.6 %collective-permute-done.1 = bf16[64,4,8,128]{3,2,1,0:T(8,128)(2,1)} collective-permute-done((bf16[64,4,8,128]{3,2,1,0:T(8,128)(2,1)}, bf16[64,4,8,128]{3,2,1,0:T(8,128)(2,1)}, u32[]{:S(2)}, u32[]{:S(2)}) %collective-permute-start.1) | collective-permute-done | bytes 524320 | tf_op jit(solution)/shard_map/ppermute | solution.py:25
  40.6 5.5 fusion.79
  46.2 23.6 %collective-permute-done.2 = bf16[64,4,8,128]{3,2,1,0:T(8,128)(2,1)} collective-permute-done((bf16[64,4,8,128]{3,2,1,0:T(8,128)(2,1)}, bf16[64,4,8,128]{3,2,1,0:T(8,128)(2,1)}, u32[]{:S(2)}, u32[]{:S(2)}) %collective-permute-start.2) | collective-permute-done | bytes 524320 | tf_op jit(solution)/shard_map/ppermute | solution.py:25
  77.1 42.0 %collective-permute-done.3 = bf16[64,4,8,128]{3,2,1,0:T(8,128)(2,1)} collective-permute-done((bf16[64,4,8,128]{3,2,1,0:T(8,128)(2,1)}, bf16[64,4,8,128]{3,2,1,0:T(8,128)(2,1)}, u32[]{:S(2)}, u32[]{:S(2)}) %collective-permute-start.3) | collective-permute-done | bytes 524320 | tf_op jit(solution)/shard_map/ppermute | solution.py:25
  125.7 16.5 %reshape.276 = bf16[16,128,4,128]{3,2,1,0:T(4,128)(2,1)} reshape(bf16[2048,512]{1,0:T(8,128)(2,1)} %get-tuple-element.759) | data formatting | bytes 4194304 | tf_op jit(solution)/shard_map/reshape | solution.py:206
  148.3 193.1 %while.59 = (s32[]{:T(128)}, f32[4,8,64]{2,1,0:T(8,128)S(1)}, f32[4,8,64]{2,1,0:T(8,128)S(1)}, f32[4,8,64,128]{3,2,1,0:T(8,128)S(1)}, f32[4,8,64]{2,1,0:T(8,128)...) while((s32[]{:T(128)}, f32[4,8,64]{2,1,0:T(8,128)S(1)}, ...), condition=%wide.region_17.18_spmd.clone, body=%wide.region_0.17_spmd.clone.sunk | while | flops 291086528 | bytes 14226523 | solution.py:227
  345.4 64.2 %all-gather.1 = bf16[64,8,128]{2,1,0:T(8,128)(2,1)} all-gather(bf16[4,8,128]{2,1,0:T(8,128)(2,1)S(1)} %fusion.143), channel_id=3, replica_groups=mesh['ctx'=16,'head'=2] {'ctx'}, dimensions={0}, use_global_device_ids=true | all-gather | bytes 139264 | tf_op jit(solution)/shard_map/all_gather | solution.py:31
  418.2 4.7 fusion.109
  422.9 4.8 collective-permute-done.5
  430.1 11.1 %collective-permute-done.6 = bf16[4,8,64,128]{3,2,1,0:T(8,128)(2,1)S(1)} collective-permute-done((bf16[4,8,64,128]{3,2,1,0:T(8,128)(2,1)S(1)}, bf16[4,8,64,128]{3,2,1,0:T(8,128)(2,1)S(1)}, u32[]{:S(2)}, u32[]{:S(2)}) %collective-permute-start.6) | collective-permute-done | bytes 524320 | tf_op jit(solution)/shard_map/ppermute | solution.py:25
  442.5 5.2 fusion.122
  447.7 18.1 %collective-permute-done.7 = bf16[4,8,64,128]{3,2,1,0:T(8,128)(2,1)S(1)} collective-permute-done((bf16[4,8,64,128]{3,2,1,0:T(8,128)(2,1)S(1)}, bf16[4,8,64,128]{3,2,1,0:T(8,128)(2,1)S(1)}, u32[]{:S(2)}, u32[]{:S(2)}) %collective-permute-start.7) | collective-permute-done | bytes 524320 | tf_op jit(solution)/shard_map/ppermute | solution.py:25
  466.8 49.1 %while.60 = (s32[]{:T(128)}, f32[4,8,128,128]{3,2,1,0:T(8,128)S(1)}, f32[4,8,128]{2,1,0:T(8,128)S(1)}, s32[]{:T(128)}, bf16[16,4,8,128,128]{4,3,2,1,0:T(8,128)(2...) while((s32[]{:T(128)}, f32[4,8,128,128]{3,2,1,0:T(8,128)S(1)}, ...), condition=%wide.region_21.22_spmd.clone, body=%wide.region_20.21_spmd.clone.sunk | while | flops 2113540 | bytes 5283955 | solution.py:48
  515.9 5.7 fusion.151
  521.7 6.4 multiply_reduce_fusion
  538.1 19.2 %all-gather.3 = bf16[64,8,128]{2,1,0:T(8,128)(2,1)S(1)} all-gather(bf16[4,8,128]{2,1,0:T(8,128)(2,1)S(1)} %convert_element_type.142), channel_id=5, replica_groups=mesh['ctx'=16,'head'=2] {'ctx'}, dimensions={0}, use_global_device_ids=true | all-gather | bytes 139264 | tf_op jit(solution)/shard_map/all_gather | solution.py:54
  560.6 7.9 fusion.68
  568.5 4.8 multiply_add_fusion.4
  577.8 81.3 %all-gather.12.cloned.1.call-done = bf16[64,8,128,128]{3,2,1,0:T(8,128)(2,1)} async-done(((bf16[4,8,128,128]{3,2,1,0:T(8,128)(2,1)}), bf16[64,8,128,128]{3,2,1,0:T(8,128)(2,1)}) %all-gather.12.cloned.1.call-update) | async-done | bytes 16777232 | tf_op jit(solution)/shard_map/all_gather | solution.py:54
  659.2 38.6 %while.61 = (s32[]{:T(128)}, f32[4,8,128,128]{3,2,1,0:T(8,128)S(1)}, f32[4,8,128]{2,1,0:T(8,128)S(1)}, s32[]{:T(128)}, bf16[16,4,8,128,128]{4,3,2,1,0:T(8,128)(2...) while((s32[]{:T(128)}, ...), condition=%wide.region_27.28_spmd.clone, body=%wide.region_26.27_spmd.clone.sunk | while | flops 2113544 | bytes 5284017 | solution.py:72
  699.4 5.7 pad_add_fusion
  705.1 5.3 fusion.102
  710.4 39.0 %psum.14 = f32[]{:T(128)} all-reduce(f32[]{:T(128)} %get-tuple-element.673), channel_id=1, replica_groups=mesh['ctx'=16,'head'=2] {'ctx','head'}, use_global_device_ids=true, to_apply=%region_24.25 | all-reduce | flops 1 | bytes 8 | tf_op jit(solution)/shard_map/psum | solution.py:276
  753.8 48.3 %all-reduce.3.cloned.1.call-done = f32[32,128,64]{1,2,0:T(8,128)} async-done(((f32[32,128,64]{1,2,0:T(8,128)}), f32[32,128,64]{1,2,0:T(8,128)}) %all-reduce.3.cloned.1.call-update) | async-done | bytes 1048592 | tf_op jit(solution)/shard_map/psum | solution.py:305
  (490 shorter events, 353.3 us)
Async XLA Ops:
  7.2 114.0 %all-gather.8.cloned.1.call-start = ((), (), s32[]{:S(2)}) async-start(), calls=%async_computation | async-start | bytes 4456448 | tf_op jit(solution)/shard_map/all_gather | solution.py:19
  9.0 457.8 %all-gather.10.cloned.1.call-start = ((), (), s32[]{:S(2)}) async-start(), calls=%async_computation.2 | async-start | bytes 17825792 | tf_op jit(solution)/shard_map/all_gather | solution.py:31
  11.1 60.9 %copy-start.22 = (bf16[128,512]{0,1:T(8,128)(2,1)}, bf16[128,512]{0,1:T(8,128)(2,1)S(1)}, u32[]{:S(2)}) copy-start(bf16[128,512]{0,1:T(8,128)(2,1)S(1)} %copy.138) | copy-start | bytes 393220
  18.2 640.9 %all-gather.12.cloned.1.call-start = ((), (), s32[]{:S(2)}) async-start(), calls=%async_computation.3 | async-start | bytes 17825792 | tf_op jit(solution)/shard_map/all_gather | solution.py:54
  20.5 3.0 collective-permute-start
  23.4 15.4 %collective-permute-start.1 = (bf16[64,4,8,128]{3,2,1,0:T(8,128)(2,1)}, bf16[64,4,8,128]{3,2,1,0:T(8,128)(2,1)}, u32[]{:S(2)}, u32[]{:S(2)}) collective-permute-start(bf16[64,4,8,128]{3,2,1,0:T(8,128)(2,1)} %collective-permute-done), channel_id=1, source_target_pairs={{0,4},{2,6},{4,0},{6,2},{8,12},{10,14},{12,8},{14,10},{16,20},{18,... | collective-permute-start | bytes 1572872 | tf_op jit(solution)/shard_map/ppermute | solution.py:25
  30.2 16.0 %copy-start.28 = (u8[4,128,64]{2,1,0:T(8,128)(4,1)}, u8[4,128,64]{2,1,0:T(8,128)(4,1)S(1)}, u32[]{:S(2)}) copy-start(u8[4,128,64]{2,1,0:T(8,128)(4,1)S(1)} %get-tuple-element.671) | copy-start | bytes 98308
  38.8 31.0 %collective-permute-start.2 = (bf16[64,4,8,128]{3,2,1,0:T(8,128)(2,1)}, bf16[64,4,8,128]{3,2,1,0:T(8,128)(2,1)}, u32[]{:S(2)}, u32[]{:S(2)}) collective-permute-start(bf16[64,4,8,128]{3,2,1,0:T(8,128)(2,1)} %collective-permute-done.1), channel_id=1, source_target_pairs={{0,8},{2,10},{4,12},{6,14},{8,0},{10,2},{12,4},{14,6},{16,24},{18,... | collective-permute-start | bytes 1572872 | tf_op jit(solution)/shard_map/ppermute | solution.py:25
  40.6 29.6 %copy-start.14 = (f32[4,8,128,64]{3,2,1,0:T(8,128)S(1)}, f32[4,8,128,64]{3,2,1,0:T(8,128)}, u32[]{:S(2)}) copy-start(f32[4,8,128,64]{3,2,1,0:T(8,128)} %copy-done.13) | copy-start | bytes 3145732
  69.8 49.3 %collective-permute-start.3 = (bf16[64,4,8,128]{3,2,1,0:T(8,128)(2,1)}, bf16[64,4,8,128]{3,2,1,0:T(8,128)(2,1)}, u32[]{:S(2)}, u32[]{:S(2)}) collective-permute-start(bf16[64,4,8,128]{3,2,1,0:T(8,128)(2,1)} %collective-permute-done.2), channel_id=1, source_target_pairs={{0,16},{2,18},{4,20},{6,22},{8,24},{10,26},{12,28},{14,30},{16,0},... | collective-permute-start | bytes 1572872 | tf_op jit(solution)/shard_map/ppermute | solution.py:25
  342.5 71.0 %collective-permute-start.4 = (bf16[4,8,64,128]{3,2,1,0:T(8,128)(2,1)}, bf16[4,8,64,128]{3,2,1,0:T(8,128)(2,1)S(1)}, u32[]{:S(2)}, u32[]{:S(2)}) collective-permute-start(bf16[4,8,64,128]{3,2,1,0:T(8,128)(2,1)} %divide_convert_fusion), channel_id=1, source_target_pairs={{0,2},{2,0},{4,6},{6,4},{8,10},{10,8},{12,14},{14,12},{16,18},{18,... | collective-permute-start | bytes 1572872 | tf_op jit(solution)/shard_map/ppermute | solution.py:25
  413.5 14.2 %collective-permute-start.5 = (bf16[4,8,64,128]{3,2,1,0:T(8,128)(2,1)S(1)}, bf16[4,8,64,128]{3,2,1,0:T(8,128)(2,1)S(1)}, u32[]{:S(2)}, u32[]{:S(2)}) collective-permute-start(bf16[4,8,64,128]{3,2,1,0:T(8,128)(2,1)S(1)} %collective-permute-done.4), channel_id=1, source_target_pairs={{0,4},{2,6},{4,0},{6,2},{8,12},{10,14},{12,8},{14,10},{16,20},{18,... | collective-permute-start | bytes 1572872 | tf_op jit(solution)/shard_map/ppermute | solution.py:25
  418.2 9.6 %copy-start.20 = (bf16[16,8,32,128]{3,2,1,0:T(8,128)(2,1)S(1)}, bf16[16,8,32,128]{3,2,1,0:T(8,128)(2,1)}, u32[]{:S(2)}) copy-start(bf16[16,8,32,128]{3,2,1,0:T(8,128)(2,1)} %copy.204) | copy-start | bytes 3145732
  418.2 9.5 %copy-start.27 = (bf16[128,4,128]{2,0,1:T(8,128)(2,1)S(1)}, bf16[128,4,128]{2,0,1:T(8,128)(2,1)}, u32[]{:S(2)}) copy-start(bf16[128,4,128]{2,0,1:T(8,128)(2,1)} %copy.128) | copy-start | bytes 393220
  427.8 13.4 %collective-permute-start.6 = (bf16[4,8,64,128]{3,2,1,0:T(8,128)(2,1)S(1)}, bf16[4,8,64,128]{3,2,1,0:T(8,128)(2,1)S(1)}, u32[]{:S(2)}, u32[]{:S(2)}) collective-permute-start(bf16[4,8,64,128]{3,2,1,0:T(8,128)(2,1)S(1)} %collective-permute-done.5), channel_id=1, source_target_pairs={{0,8},{2,10},{4,12},{6,14},{8,0},{10,2},{12,4},{14,6},{16,24},{18,... | collective-permute-start | bytes 1572872 | tf_op jit(solution)/shard_map/ppermute | solution.py:25
  430.1 12.4 %copy-start.26 = (bf16[128,4,128]{2,0,1:T(8,128)(2,1)S(1)}, bf16[128,4,128]{2,0,1:T(8,128)(2,1)}, u32[]{:S(2)}) copy-start(bf16[128,4,128]{2,0,1:T(8,128)(2,1)} %copy.139) | copy-start | bytes 393220
  441.1 24.6 %collective-permute-start.7 = (bf16[4,8,64,128]{3,2,1,0:T(8,128)(2,1)S(1)}, bf16[4,8,64,128]{3,2,1,0:T(8,128)(2,1)S(1)}, u32[]{:S(2)}, u32[]{:S(2)}) collective-permute-start(bf16[4,8,64,128]{3,2,1,0:T(8,128)(2,1)S(1)} %collective-permute-done.6), channel_id=1, source_target_pairs={{0,16},{2,18},{4,20},{6,22},{8,24},{10,26},{12,28},{14,30},{16,0},... | collective-permute-start | bytes 1572872 | tf_op jit(solution)/shard_map/ppermute | solution.py:25
  442.5 24.3 %copy-start.2 = (f32[4,8,128,128]{3,2,1,0:T(8,128)S(1)}, f32[4,8,128,128]{3,2,1,0:T(8,128)}, u32[]{:S(2)}) copy-start(f32[4,8,128,128]{3,2,1,0:T(8,128)} %custom-call) | copy-start | bytes 6291460
  515.9 12.1 %copy-start.3 = (f32[4,8,128,128]{3,2,1,0:T(8,128)}, f32[4,8,128,128]{3,2,1,0:T(8,128)S(1)}, u32[]{:S(2)}) copy-start(f32[4,8,128,128]{3,2,1,0:T(8,128)S(1)} %get-tuple-element.496) | copy-start | bytes 6291460
  534.0 268.1 %all-reduce.3.cloned.1.call-start = ((), (), s32[]{:S(2)}) async-start(), calls=%async_computation.1 | async-start | bytes 2097152 | tf_op jit(solution)/shard_map/psum | solution.py:305
  534.5 26.0 %copy-start.11 = (f32[4,8,192,64]{3,2,1,0:T(8,128)S(1)}, f32[4,8,192,64]{3,2,1,0:T(8,128)}, u32[]{:S(2)}) copy-start(f32[4,8,192,64]{3,2,1,0:T(8,128)} %copy-done.10) | copy-start | bytes 4718596
  560.5 7.9 copy-start.12
  659.2 38.6 %copy-start.23 = (bf16[128,512]{0,1:T(8,128)(2,1)S(1)}, bf16[128,512]{0,1:T(8,128)(2,1)}, u32[]{:S(2)}) copy-start(bf16[128,512]{0,1:T(8,128)(2,1)} %copy-done.22) | copy-start | bytes 393220
  751.3 53.1 %copy-start.1 = (bf16[32,128,64]{1,2,0:T(8,128)(2,1)S(1)}, bf16[32,128,64]{1,2,0:T(8,128)(2,1)}, u32[]{:S(2)}) copy-start(bf16[32,128,64]{1,2,0:T(8,128)(2,1)} %param.21) | copy-start | bytes 1572868
  (20 other events, 93.7 us)
Sparse Core Ops, SparseCore 0:
  10.2 60.3 all-gather.7
  72.7 137.4 all-gather.9
  534.1 125.0 all-gather.11
  710.5 91.5 all-reduce.2
